TPU v7x, 32 devices: a whole 2x2x4 slice. The times are simulated.
32 devices in a mesh: seq: 8 (over y, x, core), head: 4 (over z).
Axes of the slice: x: 2, y: 2, z: 4, core: 2. Of those that a mesh axis runs over, the one named last changes fastest.
Arguments:
- queries: bfloat16 [2, 8, 8, 32, 128], P(None, 'head'), may hold values from -128 to 128
- tree_keys: bfloat16 [2, 8, 32, 128], P(None, 'head'), may hold values from -8 to 8
- tree_values: bfloat16 [2, 8, 32, 128], P(None, 'head'), may hold values from -6 to 6
- cache_keys: bfloat16 [8, 8192, 128], P('head', 'seq'), may hold values from -6 to 6
- cache_values: bfloat16 [8, 8192, 128], P('head', 'seq'), may hold values from -6 to 6
- block_ids: int32 [8, 32], P('head'), may hold values from 0 to 63, as said below
- ancestors: int32 [1, 32, 32], replicated, may hold values from 0 to 1, as said below
- out_weight: bfloat16 [8192, 8192], P('seq', 'head'), may hold values from -0.0625 to 0.0625
Outputs:
- draft_mixed: bfloat16 [32, 1, 8192], P('seq', None, 'head')
- verify_mixed: bfloat16 [32, 1, 8192], P('seq', None, 'head')
Inputs may be any that keep to these rules, and one draw needn't show every extreme that they name: `block_ids`: the 32 block numbers of one pair are distinct, and for every pair one run of 1024 positions (positions s * 1024 to (s + 1) * 1024 - 1 for some s) holds at least half of its 32 blocks, or all 8 blocks of the run where the run has fewer. ancestors[r, n, k] is 1 exactly when k is n or an ancestor of n in request r's tree; node 0 is the root and every other node's parent has a smaller number.
All inputs are finite; a program needn't handle non-finite values.
Results may differ from a plain program's by a relative error of at most 0.009.
Values may be sent and summed in bfloat16 or wider, within the bound.
A program may use at most 64 MiB of HBM per device.

v0:
```python
import jax
import jax.numpy as jnp
from jax import lax
from jax.sharding import PartitionSpec as P

KVH = 8
BLOCK = 128


def cache_partial(query_rows, key_rows, value_rows, chosen_mask, score_scale):
    scores = (
        jnp.einsum("pgnh,plh->pgnl", query_rows, key_rows, preferred_element_type=jnp.float32)
        * score_scale
    )
    if chosen_mask is not None:
        scores = jnp.where(chosen_mask[:, None, None, :], scores, -1e30)
    peaks = jnp.max(scores, axis=-1)
    weights = jnp.exp(scores - peaks[..., None])
    if chosen_mask is not None:
        weights = jnp.where(chosen_mask[:, None, None, :], weights, 0.0)
    totals = jnp.sum(weights, axis=-1)
    summed = jnp.einsum(
        "pgnl,plh->pgnh",
        weights.astype(jnp.bfloat16),
        value_rows,
        preferred_element_type=jnp.float32,
    )
    return (peaks, totals, summed)


def tree_partial(query_rows, tree_key_rows, tree_value_rows, tree_mask, score_scale):
    scores = (
        jnp.einsum("pgnh,pkh->pgnk", query_rows, tree_key_rows, preferred_element_type=jnp.float32)
        * score_scale
    )
    allowed = tree_mask[:, None] > 0
    scores = jnp.where(allowed, scores, -1e30)
    peaks = jnp.max(scores, axis=-1)
    weights = jnp.where(allowed, jnp.exp(scores - peaks[..., None]), 0.0)
    totals = jnp.sum(weights, axis=-1)
    summed = jnp.einsum(
        "pgnk,pkh->pgnh",
        weights.astype(jnp.bfloat16),
        tree_value_rows,
        preferred_element_type=jnp.float32,
    )
    return (peaks, totals, summed)


def combine_two(first_part, second_part):
    peaks = jnp.maximum(first_part[0], second_part[0])
    first_factor = jnp.exp(first_part[0] - peaks)
    second_factor = jnp.exp(second_part[0] - peaks)
    totals = first_part[1] * first_factor + second_part[1] * second_factor
    summed = first_part[2] * first_factor[..., None] + second_part[2] * second_factor[..., None]
    return (peaks, totals, summed)


def combine_over(peaks, totals, summed):
    highest = jnp.max(peaks, axis=0)
    factor = jnp.exp(peaks - highest[None])
    return (highest, jnp.sum(totals * factor, axis=0), jnp.sum(summed * factor[..., None], axis=0))


def finish(cache_part, tree_part):
    peaks, totals, summed = combine_two(cache_part, tree_part)
    result = summed / totals[..., None]
    pair_count, groups, node_count, head_dim = result.shape
    return (
        jnp.transpose(result, (0, 2, 1, 3))
        .reshape(pair_count, node_count, groups * head_dim)
        .astype(jnp.bfloat16)
    )


def local(
    queries, tree_keys, tree_values, cache_keys, cache_values, block_ids, ancestors, out_weight
):
    pair_dev, ctx_dev, head_dim = cache_keys.shape
    groups = queries.shape[2]
    node_count = queries.shape[3]
    requests = ancestors.shape[0]
    score_scale = head_dim ** (-0.5)
    seq_count = lax.axis_size("seq")
    seq_index = lax.axis_index("seq")
    head_index = lax.axis_index("head")
    blocks_dev = ctx_dev // BLOCK
    node_dev = node_count // seq_count
    pair_ids = head_index * pair_dev + jnp.arange(pair_dev, dtype=jnp.int32)
    picker = (pair_ids[:, None] // KVH == jnp.arange(requests, dtype=jnp.int32)[None, :]).astype(
        jnp.int32
    )
    tree_masks = jnp.sum(picker[:, :, None, None] * ancestors[None], axis=1)
    verify_part = cache_partial(queries[1], cache_keys, cache_values, None, score_scale)
    owned_ids = seq_index * blocks_dev + jnp.arange(blocks_dev, dtype=jnp.int32)
    chosen = jnp.any(block_ids[:, :, None] == owned_ids[None, None, :], axis=1)
    chosen_mask = jnp.broadcast_to(chosen[:, :, None], (pair_dev, blocks_dev, BLOCK)).reshape(
        pair_dev, ctx_dev
    )
    draft_part = cache_partial(queries[0], cache_keys, cache_values, chosen_mask, score_scale)
    arrived = (
        lax.all_to_all(draft_part[0][None], "seq", split_axis=3, concat_axis=0, tiled=True),
        lax.all_to_all(draft_part[1][None], "seq", split_axis=3, concat_axis=0, tiled=True),
        lax.all_to_all(draft_part[2][None], "seq", split_axis=3, concat_axis=0, tiled=True),
        lax.all_to_all(verify_part[0][None], "seq", split_axis=3, concat_axis=0, tiled=True),
        lax.all_to_all(verify_part[1][None], "seq", split_axis=3, concat_axis=0, tiled=True),
        lax.all_to_all(verify_part[2][None], "seq", split_axis=3, concat_axis=0, tiled=True),
    )
    draft_cache = combine_over(arrived[0], arrived[1], arrived[2])
    verify_cache = combine_over(arrived[3], arrived[4], arrived[5])
    row_start = seq_index * node_dev
    mask_rows = lax.dynamic_slice_in_dim(tree_masks, row_start, node_dev, 1)
    draft_tree = tree_partial(
        lax.dynamic_slice_in_dim(queries[0], row_start, node_dev, 2),
        tree_keys[0],
        tree_values[0],
        mask_rows,
        score_scale,
    )
    verify_tree = tree_partial(
        lax.dynamic_slice_in_dim(queries[1], row_start, node_dev, 2),
        tree_keys[1],
        tree_values[1],
        mask_rows,
        score_scale,
    )
    draft_all, verify_all = (
        lax.all_gather(finish(draft_cache, draft_tree), "seq", axis=1, tiled=True),
        lax.all_gather(finish(verify_cache, verify_tree), "seq", axis=1, tiled=True),
    )
    gathered = (
        lax.all_gather(draft_all, "head", axis=0, tiled=True),
        lax.all_gather(verify_all, "head", axis=0, tiled=True),
    )
    stacked = jnp.stack(gathered)
    stacked = stacked.reshape(2, requests, KVH, node_count, groups * head_dim)
    stacked = jnp.transpose(stacked, (3, 0, 1, 2, 4)).reshape(
        node_count, 2 * requests, KVH * groups * head_dim
    )
    rows_dev = out_weight.shape[0]
    columns = lax.dynamic_slice_in_dim(stacked, seq_index * rows_dev, rows_dev, 2)
    own_rows = lax.psum_scatter(
        jnp.einsum("nrk,kd->nrd", columns, out_weight, preferred_element_type=jnp.float32),
        "seq",
        scatter_dimension=0,
        tiled=True,
    )
    own_rows = own_rows.reshape(node_dev, 2, requests, own_rows.shape[-1]).astype(jnp.bfloat16)
    return (own_rows[:, 0], own_rows[:, 1])


def solution(mesh):
    in_specs = (
        P(None, "head", None, None, None),
        P(None, "head", None, None),
        P(None, "head", None, None),
        P("head", "seq", None),
        P("head", "seq", None),
        P("head", None),
        P(),
        P("seq", "head"),
    )
    out_specs = (P("seq", None, "head"), P("seq", None, "head"))
    return jax.shard_map(local, mesh=mesh, in_specs=in_specs, out_specs=out_specs, check_vma=False)
```

profile of v0, /device:TPU:0, one launch (start us, length us, event | category | flops | bytes accessed | tf_op | source)
XLA Modules:
  0.0 145.6 jit_solution(11215316324020661436)
XLA Ops:
  0.6 0.0 copy-start
  0.7 0.9 compare_reduce_fusion
  1.6 0.1 broadcast_bitcast_fusion
  1.7 0.0 copy-start.5
  1.7 0.0 copy-done
  1.7 1.5 %fusion.2 = (f32[2,8,32]{2,1,0:T(8,128)S(1)}, f32[2,8,32,1024]{3,2,1,0:T(8,128)S(1)}) fusion(pred[2,1024]{1,0:T(4,128)(4,1)S(1)} %bitcast.216, bf16[2,1024,128]{2,1,0:T(8,128)(2,1)S(1)} %copy-done, bf16[2,2,8,32,128]{4,3,2,1,0:T(8,128)(2,1)} %param.8), kind=kOutput, calls=%fused_computation.6 | convolution fusion | flops 135790080 | bytes 2756608 | tf_op jit(solution)/shard_map/pgnh,plh->pgnl/dot_general | solution.py:12
  3.2 0.0 copy-start.1
  3.2 0.0 copy-done.5
  3.2 1.3 copy-done.1
  4.5 0.6 fusion.5
  5.2 0.7 copy.50
  5.9 5.2 %all-to-all-start.2 = ((f32[1,2,8,32]{2,1,0,3:T(2,128)}), f32[1,2,8,32]{2,1,0,3:T(2,128)}, u32[]{:S(2)}, u32[]{:S(2)}) async-start(f32[1,2,8,32]{2,1,0,3:T(2,128)} %copy.50), calls=%async_computation.2 | async-start | bytes 65536 | tf_op jit(solution)/shard_map/all_to_all | solution.py:103
  11.1 0.0 copy-done.2
  11.1 0.7 fusion.81
  11.8 0.5 multiply_reduce_fusion
  12.3 0.0 copy-done.3
  12.3 3.0 %convolution_bitcast_fusion.1 = f32[1,2,8,32,128]{4,3,2,1,0:T(8,128)} fusion(f32[2,8,32,1024]{3,2,1,0:T(8,128)} %copy-done.1, f32[2,8,32]{2,1,0:T(8,128)S(1)} %get-tuple-element.24, pred[2,1024]{1,0:T(4,128)(4,1)} %bitcast.218, bf16[2,1024,128]{2,1,0:T(8,128)(2,1)S(1)} %copy-done.3), kind=kOutput, calls=%fused_computation.12 | convolution fusion | flops 136839168 | bytes 2887680 | tf_op jit(solution)/shard_map/pgnl,plh->pgnh/dot_general | solution.py:22
  15.3 0.7 constant_dynamic-slice_fusion.2
  16.0 0.1 fusion.67
  16.1 0.8 constant_dynamic-slice_fusion
  16.8 0.6 convolution_bitcast_fusion
  17.4 0.0 copy-start.4
  17.4 0.0 copy-start.10
  17.4 0.2 fusion.83
  17.7 0.2 fusion.82
  17.9 0.0 copy-done.7
  17.9 0.0 copy-start.8
  17.9 0.7 copy.45
  18.6 0.0 all-to-all-done.2
  18.6 4.2 %all-to-all-start.1 = ((f32[1,2,8,32]{2,1,0,3:T(2,128)}), f32[1,2,8,32]{2,1,0,3:T(2,128)S(1)}, u32[]{:S(2)}, u32[]{:S(2)}) async-start(f32[1,2,8,32]{2,1,0,3:T(2,128)} %copy.45), calls=%async_computation.1 | async-start | bytes 65536 | tf_op jit(solution)/shard_map/all_to_all | solution.py:102
  22.8 0.5 fusion.3
  23.3 0.0 copy-start.9
  23.3 0.7 copy.56
  24.0 3.6 %all-to-all-done.1 = f32[1,2,8,32]{2,1,0,3:T(2,128)S(1)} async-done(((f32[1,2,8,32]{2,1,0,3:T(2,128)}), f32[1,2,8,32]{2,1,0,3:T(2,128)S(1)}, u32[]{:S(2)}, u32[]{:S(2)}) %all-to-all-start.1) | async-done | bytes 2080 | tf_op jit(solution)/shard_map/all_to_all | solution.py:102
  27.6 3.3 %all-to-all-start.4 = ((f32[1,2,8,32]{2,1,0,3:T(2,128)}), f32[1,2,8,32]{2,1,0,3:T(2,128)S(1)}, u32[]{:S(2)}, u32[]{:S(2)}) async-start(f32[1,2,8,32]{2,1,0,3:T(2,128)} %copy.56), calls=%async_computation.4 | async-start | bytes 65536 | tf_op jit(solution)/shard_map/all_to_all | solution.py:105
  31.0 0.2 fusion.37
  31.2 0.9 copy.43
  32.0 0.8 copy.54
  32.9 0.7 copy.61
  33.6 0.6 dynamic-slice.3
  34.8 0.8 copy.51
  35.6 0.1 all-to-all-done.4
  35.7 4.0 %all-to-all-start.5 = ((f32[1,2,8,32]{2,1,0,3:T(2,128)}), f32[1,2,8,32]{2,1,0,3:T(2,128)S(1)}, u32[]{:S(2)}, u32[]{:S(2)}) async-start(f32[1,2,8,32]{2,1,0,3:T(2,128)} %copy.61), calls=%async_computation.5 | async-start | bytes 65536 | tf_op jit(solution)/shard_map/all_to_all | solution.py:106
  39.8 4.8 %all-to-all-done.5 = f32[1,2,8,32]{2,1,0,3:T(2,128)S(1)} async-done(((f32[1,2,8,32]{2,1,0,3:T(2,128)}), f32[1,2,8,32]{2,1,0,3:T(2,128)S(1)}, u32[]{:S(2)}, u32[]{:S(2)}) %all-to-all-start.5) | async-done | bytes 2080 | tf_op jit(solution)/shard_map/all_to_all | solution.py:106
  44.6 3.4 %all-to-all-start = ((f32[1,2,8,32,128]{4,2,1,0,3:T(8,128)}), f32[1,2,8,32,128]{4,2,1,0,3:T(8,128)S(1)}, u32[]{:S(2)}, u32[]{:S(2)}) async-start(f32[1,2,8,32,128]{4,2,1,0,3:T(8,128)} %copy.43), calls=%async_computation | async-start | bytes 524288 | tf_op jit(solution)/shard_map/all_to_all | solution.py:104
  48.1 0.2 copy.47
  48.2 0.2 copy.58
  48.4 6.4 %all-to-all-done = f32[1,2,8,32,128]{4,2,1,0,3:T(8,128)S(1)} async-done(((f32[1,2,8,32,128]{4,2,1,0,3:T(8,128)}), f32[1,2,8,32,128]{4,2,1,0,3:T(8,128)S(1)}, u32[]{:S(2)}, u32[]{:S(2)}) %all-to-all-start) | async-done | bytes 262176 | tf_op jit(solution)/shard_map/all_to_all | solution.py:104
  54.8 3.4 %all-to-all-start.3 = ((f32[1,2,8,32,128]{4,2,1,0,3:T(8,128)}), f32[1,2,8,32,128]{4,2,1,0,3:T(8,128)S(1)}, u32[]{:S(2)}, u32[]{:S(2)}) async-start(f32[1,2,8,32,128]{4,2,1,0,3:T(8,128)} %copy.54), calls=%async_computation.3 | async-start | bytes 524288 | tf_op jit(solution)/shard_map/all_to_all | solution.py:107
  58.2 0.2 fusion.32
  58.5 0.2 fusion.15
  58.7 9.8 %all_gather.12 = bf16[2,32,1024]{2,0,1:T(2,128)(2,1)S(1)} all-gather(bf16[2,4,1024]{2,0,1:T(2,128)(2,1)S(1)} %copy.52), channel_id=1, replica_groups=mesh['seq'=8,'head'=4] {'seq'}, dimensions={1}, use_global_device_ids=true | all-gather | bytes 147456 | tf_op jit(solution)/shard_map/all_gather | solution.py:128
  68.6 16.5 %all_gather.13 = bf16[8,32,1024]{2,1,0:T(8,128)(2,1)S(1)} all-gather(bf16[2,32,1024]{2,1,0:T(8,128)(2,1)S(1)} %copy.53), channel_id=1, replica_groups=mesh['seq'=8,'head'=4] {'head'}, dimensions={0}, use_global_device_ids=true | all-gather | bytes 655360 | tf_op jit(solution)/shard_map/all_gather | solution.py:132
  85.0 0.0 all-to-all-done.3
  85.0 0.2 fusion.31
  85.3 0.2 fusion.16
  85.5 9.2 %all_gather.14 = bf16[2,32,1024]{2,0,1:T(2,128)(2,1)S(1)} all-gather(bf16[2,4,1024]{2,0,1:T(2,128)(2,1)S(1)} %copy.63), channel_id=1, replica_groups=mesh['seq'=8,'head'=4] {'seq'}, dimensions={1}, use_global_device_ids=true | all-gather | bytes 147456 | tf_op jit(solution)/shard_map/all_gather | solution.py:129
  94.7 16.5 %all_gather.15 = bf16[8,32,1024]{2,1,0:T(8,128)(2,1)S(1)} all-gather(bf16[2,32,1024]{2,1,0:T(8,128)(2,1)S(1)} %copy.64), channel_id=1, replica_groups=mesh['seq'=8,'head'=4] {'head'}, dimensions={0}, use_global_device_ids=true | all-gather | bytes 655360 | tf_op jit(solution)/shard_map/all_gather | solution.py:133
  111.2 0.1 maximum_bitcast_fusion
  111.3 0.6 copy.65
  111.9 0.5 reshape.148
  112.4 3.0 %fusion = f32[32,2,2048]{2,0,1:T(8,128)S(1)} fusion(bf16[1024,2048]{1,0:T(8,128)(2,1)} %param.15, bf16[32,2,8192]{2,0,1:T(8,128)(2,1)S(1)} %reshape.148, s32[]{:T(128)S(6)} %select_n.47), kind=kOutput, calls=%fused_computation | convolution fusion | flops 268435456 | bytes 4849668 | tf_op jit(solution)/shard_map/nrk,kd->nrd/dot_general | solution.py:143
  115.5 29.5 %all-reduce.2 = bf16[32,2,2048]{2,0,1:T(8,128)(2,1)S(1)} all-reduce(f32[32,2,2048]{2,0,1:T(8,128)S(1)} %fusion), channel_id=2, replica_groups=mesh['seq'=8,'head'=4] {'seq'}, use_global_device_ids=true, to_apply=%region_15.16.clone | all-reduce | flops 131072 | bytes 786432
  145.0 0.6 slice_bitcast_fusion
  (28 shorter events, 0.3 us)
Async XLA Ops:
  0.6 1.1 copy-start
  1.7 1.5 %copy-start.5 = (pred[1,2,8,128]{3,1,2,0:T(4,128)(4,1)}, pred[1,2,8,128]{3,1,2,0:T(4,128)(4,1)S(1)}, u32[]{:S(2)}) copy-start(pred[1,2,8,128]{3,1,2,0:T(4,128)(4,1)S(1)} %copy.92) | copy-start | bytes 6148
  1.7 9.4 %copy-start.2 = (bf16[2,2,8,32,128]{4,3,2,1,0:T(8,128)(2,1)S(1)}, bf16[2,2,8,32,128]{4,3,2,1,0:T(8,128)(2,1)}, u32[]{:S(2)}) copy-start(bf16[2,2,8,32,128]{4,3,2,1,0:T(8,128)(2,1)} %param.8) | copy-start | bytes 786436
  3.2 1.4 copy-start.1
  5.2 7.1 %copy-start.3 = (bf16[2,1024,128]{2,1,0:T(8,128)(2,1)S(1)}, bf16[2,1024,128]{2,1,0:T(8,128)(2,1)}, u32[]{:S(2)}) copy-start(bf16[2,1024,128]{2,1,0:T(8,128)(2,1)} %param.12) | copy-start | bytes 1572868
  5.9 12.7 %all-to-all-start.2 = ((f32[1,2,8,32]{2,1,0,3:T(2,128)}), f32[1,2,8,32]{2,1,0,3:T(2,128)}, u32[]{:S(2)}, u32[]{:S(2)}) async-start(f32[1,2,8,32]{2,1,0,3:T(2,128)} %copy.50), calls=%async_computation.2 | async-start | bytes 65536 | tf_op jit(solution)/shard_map/all_to_all | solution.py:103
  15.3 2.2 %copy-start.6 = (bf16[2,2,32,128]{3,2,1,0:T(8,128)(2,1)S(1)}, bf16[2,2,32,128]{3,2,1,0:T(8,128)(2,1)}, u32[]{:S(2)}) copy-start(bf16[2,2,32,128]{3,2,1,0:T(8,128)(2,1)} %param.9) | copy-start | bytes 98308
  16.1 1.8 %copy-start.7 = (pred[2,4,32]{2,1,0:T(4,128)(4,1)}, pred[2,4,32]{2,1,0:T(4,128)(4,1)S(1)}, u32[]{:S(2)}) copy-start(pred[2,4,32]{2,1,0:T(4,128)(4,1)S(1)} %fusion.67) | copy-start | bytes 772
  17.4 13.8 %copy-start.4 = (f32[1,2,8,32,128]{4,3,2,1,0:T(8,128)S(1)}, f32[1,2,8,32,128]{4,3,2,1,0:T(8,128)}, u32[]{:S(2)}) copy-start(f32[1,2,8,32,128]{4,3,2,1,0:T(8,128)} %convolution_bitcast_fusion.1) | copy-start | bytes 786436
  17.4 16.1 %copy-start.10 = (u32[32]{0:T(128)S(1)}, u32[32]{0:T(128)}, u32[]{:S(2)}) copy-start(u32[32]{0:T(128)} %constant.61) | copy-start | bytes 388
  17.9 13.1 %copy-start.8 = (pred[2,4,32]{2,1,0:T(4,128)(4,1)S(1)}, pred[2,4,32]{2,1,0:T(4,128)(4,1)}, u32[]{:S(2)}) copy-start(pred[2,4,32]{2,1,0:T(4,128)(4,1)} %copy-done.7) | copy-start | bytes 772
  18.6 9.0 %all-to-all-start.1 = ((f32[1,2,8,32]{2,1,0,3:T(2,128)}), f32[1,2,8,32]{2,1,0,3:T(2,128)S(1)}, u32[]{:S(2)}, u32[]{:S(2)}) async-start(f32[1,2,8,32]{2,1,0,3:T(2,128)} %copy.45), calls=%async_computation.1 | async-start | bytes 65536 | tf_op jit(solution)/shard_map/all_to_all | solution.py:102
  23.3 35.2 %copy-start.9 = (bf16[2,2,32,128]{3,2,1,0:T(8,128)(2,1)S(1)}, bf16[2,2,32,128]{3,2,1,0:T(8,128)(2,1)}, u32[]{:S(2)}) copy-start(bf16[2,2,32,128]{3,2,1,0:T(8,128)(2,1)} %param.10) | copy-start | bytes 98308
  27.6 8.1 %all-to-all-start.4 = ((f32[1,2,8,32]{2,1,0,3:T(2,128)}), f32[1,2,8,32]{2,1,0,3:T(2,128)S(1)}, u32[]{:S(2)}, u32[]{:S(2)}) async-start(f32[1,2,8,32]{2,1,0,3:T(2,128)} %copy.56), calls=%async_computation.4 | async-start | bytes 65536 | tf_op jit(solution)/shard_map/all_to_all | solution.py:105
  35.7 8.8 %all-to-all-start.5 = ((f32[1,2,8,32]{2,1,0,3:T(2,128)}), f32[1,2,8,32]{2,1,0,3:T(2,128)S(1)}, u32[]{:S(2)}, u32[]{:S(2)}) async-start(f32[1,2,8,32]{2,1,0,3:T(2,128)} %copy.61), calls=%async_computation.5 | async-start | bytes 65536 | tf_op jit(solution)/shard_map/all_to_all | solution.py:106
  44.6 10.3 %all-to-all-start = ((f32[1,2,8,32,128]{4,2,1,0,3:T(8,128)}), f32[1,2,8,32,128]{4,2,1,0,3:T(8,128)S(1)}, u32[]{:S(2)}, u32[]{:S(2)}) async-start(f32[1,2,8,32,128]{4,2,1,0,3:T(8,128)} %copy.43), calls=%async_computation | async-start | bytes 524288 | tf_op jit(solution)/shard_map/all_to_all | solution.py:104
  54.8 30.2 %all-to-all-start.3 = ((f32[1,2,8,32,128]{4,2,1,0,3:T(8,128)}), f32[1,2,8,32,128]{4,2,1,0,3:T(8,128)S(1)}, u32[]{:S(2)}, u32[]{:S(2)}) async-start(f32[1,2,8,32,128]{4,2,1,0,3:T(8,128)} %copy.54), calls=%async_computation.3 | async-start | bytes 524288 | tf_op jit(solution)/shard_map/all_to_all | solution.py:107
where the time goes:
time: 147 us; the launch traced here: 146 us
  blocking collectives  81.4 us (55%)
  starting transfers between devices  23.5 us (16%)
  waiting for transfers between devices  15 us (10%)
  local copies, waits for them, and re-layouts  11.7 us (8%)
  matrix products  9.38 us (6%)
  other arithmetic  2.98 us (2%)
  between operations  1.64 us (1%)
    unnamed x1, blocking collectives  29.5 us
    all_gather x1, blocking collectives, local(): lax.all_gather(verify_all, 'head', axis=0, tiled=True)  16.5 us
    all_gather x1, blocking collectives, local(): lax.all_gather(draft_all, 'head', axis=0, tiled=True)  16.5 us
    all_gather x1, blocking collectives, local(): lax.all_gather(finish(draft_cache, draft_tree), 'seq', axis=1, tiled=True)  9.83 us
    all_gather x1, blocking collectives, local(): lax.all_gather(finish(verify_cache, verify_tree), 'seq', axis=1, tiled=True)  9.17 us
    all_to_all x1, waiting for transfers between devices, local(): lax.all_to_all(draft_part[2][None], 'seq', split_axis=3, concat_axis=0, t...  6.41 us
    all_to_all x1, starting transfers between devices, local(): lax.all_to_all(draft_part[1][None], 'seq', split_axis=3, concat_axis=0, t...  5.2 us
    all_to_all x1, waiting for transfers between devices, local(): lax.all_to_all(verify_part[1][None], 'seq', split_axis=3, concat_axis=0,...  4.78 us
  transfers between devices with their start and end apart: 6, of which 4 were waited for; matrix products, arithmetic and copies ran while one was open for 9% of the time, Pallas kernels for 0%

commit v1 on v0

--- a/solution.py
+++ b/solution.py
@@ -101,7 +101,12 @@
     arrived = (
         lax.all_to_all(draft_part[0][None], "seq", split_axis=3, concat_axis=0, tiled=True),
         lax.all_to_all(draft_part[1][None], "seq", split_axis=3, concat_axis=0, tiled=True),
-        lax.all_to_all(draft_part[2][None], "seq", split_axis=3, concat_axis=0, tiled=True),
+        jnp.concatenate(
+            lax.all_to_all(
+                jnp.stack(jnp.split(draft_part[2][None], lax.axis_size("seq"), axis=3)), "seq", 0, 0
+            ),
+            axis=0,
+        ),
         lax.all_to_all(verify_part[0][None], "seq", split_axis=3, concat_axis=0, tiled=True),
         lax.all_to_all(verify_part[1][None], "seq", split_axis=3, concat_axis=0, tiled=True),
         lax.all_to_all(verify_part[2][None], "seq", split_axis=3, concat_axis=0, tiled=True),

time: 147 us -> 151 us (1.027)
  local copies, waits for them, and re-layouts: 11.7 us -> 15.7 us
    unnamed x25 -> x26, local copies, waits for them, and re-layouts: 2.07 us -> 6.35 us
  transfers between devices with their start and end apart: 6 -> 6, of which waited for: 4 -> 4; matrix products, arithmetic and copies ran while one was open for 9% -> 12% of each run, Pallas kernels for 0% -> 0%
where the time goes in v1:
time: 151 us; the launch traced here: 150 us
  blocking collectives  81.4 us (54%)
  starting transfers between devices  22.9 us (15%)
  waiting for transfers between devices  15.8 us (10%)
  local copies, waits for them, and re-layouts  15.7 us (10%)
  matrix products  9.37 us (6%)
  other arithmetic  2.99 us (2%)
  between operations  1.62 us (1%)
    unnamed x1, blocking collectives  29.5 us
    all_gather x1, blocking collectives, local(): lax.all_gather(verify_all, 'head', axis=0, tiled=True)  16.5 us
    all_gather x1, blocking collectives, local(): lax.all_gather(draft_all, 'head', axis=0, tiled=True)  16.5 us
    all_gather x1, blocking collectives, local(): lax.all_gather(finish(draft_cache, draft_tree), 'seq', axis=1, tiled=True)  9.81 us
    all_gather x1, blocking collectives, local(): lax.all_gather(finish(verify_cache, verify_tree), 'seq', axis=1, tiled=True)  9.17 us
    all_to_all x1, waiting for transfers between devices, local(): lax.all_to_all(jnp.stack(jnp.split(draft_part[2][None], lax.axis_size('se...  6.42 us
    unnamed x26, local copies, waits for them, and re-layouts  6.35 us
    all_to_all x1, starting transfers between devices, local(): lax.all_to_all(draft_part[1][None], 'seq', split_axis=3, concat_axis=0, t...  5.2 us
  transfers between devices with their start and end apart: 6, of which 4 were waited for; matrix products, arithmetic and copies ran while one was open for 12% of the time, Pallas kernels for 0%

profile of v1, /device:TPU:0, one launch (start us, length us, event | category | flops | bytes accessed | tf_op | source)
XLA Modules:
  0.0 149.8 jit_solution(18076260183175991145)
XLA Ops:
  0.6 0.0 copy-start
  0.7 0.9 compare_reduce_fusion
  1.6 0.1 broadcast_bitcast_fusion
  1.7 0.0 copy-start.4
  1.7 0.0 copy-done
  1.7 1.5 fusion.2
  3.2 1.3 copy-done.1
  4.5 0.6 fusion.5
  5.2 0.7 copy.47
  5.9 5.2 %all-to-all-start.2 = ((f32[1,2,8,32]{2,1,0,3:T(2,128)}), f32[1,2,8,32]{2,1,0,3:T(2,128)}, u32[]{:S(2)}, u32[]{:S(2)}) async-start(f32[1,2,8,32]{2,1,0,3:T(2,128)} %copy.47), calls=%async_computation.2 | async-start | bytes 65536 | tf_op jit(solution)/shard_map/all_to_all | solution.py:103
  11.1 0.7 fusion.89
  11.8 0.5 multiply_reduce_fusion
  12.3 2.2 %convolution_bitcast_fusion.1 = f32[1,2,8,32,128]{4,3,2,1,0:T(8,128)S(1)} fusion(f32[2,8,32,1024]{3,2,1,0:T(8,128)} %copy-done.1, f32[2,8,32]{2,1,0:T(8,128)S(1)} %get-tuple-element.24, pred[2,1024]{1,0:T(4,128)(4,1)} %bitcast.246, bf16[2,1024,128]{2,1,0:T(8,128)(2,1)S(1)} %copy-done.3), kind=kOutput, calls=%fused_computation.12 | convolution fusion | flops 136839168 | bytes 2887680 | tf_op jit(solution)/shard_map/pgnl,plh->pgnh/dot_general | solution.py:22
  14.6 0.0 copy-start.5
  14.6 0.6 fusion.44
  15.2 0.6 fusion.43
  15.8 0.6 fusion.42
  16.4 0.6 fusion.41
  17.0 0.6 fusion.40
  17.6 0.6 fusion.39
  18.3 0.6 fusion.38
  18.9 0.6 fusion.37
  19.5 0.7 constant_dynamic-slice_fusion.2
  20.2 0.1 fusion.75
  20.3 0.8 constant_dynamic-slice_fusion
  21.0 0.6 convolution_bitcast_fusion
  21.6 0.0 copy-start.7
  21.6 0.2 fusion.91
  21.8 0.9 fusion.90
  22.8 0.7 copy.42
  23.5 0.0 all-to-all-done.2
  23.5 4.2 %all-to-all-start.1 = ((f32[1,2,8,32]{2,1,0,3:T(2,128)}), f32[1,2,8,32]{2,1,0,3:T(2,128)S(1)}, u32[]{:S(2)}, u32[]{:S(2)}) async-start(f32[1,2,8,32]{2,1,0,3:T(2,128)} %copy.42), calls=%async_computation.1 | async-start | bytes 65536 | tf_op jit(solution)/shard_map/all_to_all | solution.py:102
  27.7 0.5 fusion.3
  28.2 0.7 copy.53
  28.9 3.6 %all-to-all-done.1 = f32[1,2,8,32]{2,1,0,3:T(2,128)S(1)} async-done(((f32[1,2,8,32]{2,1,0,3:T(2,128)}), f32[1,2,8,32]{2,1,0,3:T(2,128)S(1)}, u32[]{:S(2)}, u32[]{:S(2)}) %all-to-all-start.1) | async-done | bytes 2080 | tf_op jit(solution)/shard_map/all_to_all | solution.py:102
  32.5 3.3 %all-to-all-start.4 = ((f32[1,2,8,32]{2,1,0,3:T(2,128)}), f32[1,2,8,32]{2,1,0,3:T(2,128)S(1)}, u32[]{:S(2)}, u32[]{:S(2)}) async-start(f32[1,2,8,32]{2,1,0,3:T(2,128)} %copy.53), calls=%async_computation.4 | async-start | bytes 65536 | tf_op jit(solution)/shard_map/all_to_all | solution.py:110
  35.8 0.2 fusion.45
  36.0 0.8 copy.51
  36.9 0.7 copy.58
  37.6 0.6 dynamic-slice.3
  38.8 0.8 copy.48
  39.6 1.0 all-to-all-done.4
  40.6 3.3 %all-to-all-start.5 = ((f32[1,2,8,32]{2,1,0,3:T(2,128)}), f32[1,2,8,32]{2,1,0,3:T(2,128)S(1)}, u32[]{:S(2)}, u32[]{:S(2)}) async-start(f32[1,2,8,32]{2,1,0,3:T(2,128)} %copy.58), calls=%async_computation.5 | async-start | bytes 65536 | tf_op jit(solution)/shard_map/all_to_all | solution.py:111
  44.0 4.7 %all-to-all-done.5 = f32[1,2,8,32]{2,1,0,3:T(2,128)S(1)} async-done(((f32[1,2,8,32]{2,1,0,3:T(2,128)}), f32[1,2,8,32]{2,1,0,3:T(2,128)S(1)}, u32[]{:S(2)}, u32[]{:S(2)}) %all-to-all-start.5) | async-done | bytes 2080 | tf_op jit(solution)/shard_map/all_to_all | solution.py:111
  48.7 3.4 %all-to-all-start = ((f32[8,1,2,8,4,128]{5,4,3,2,1,0:T(4,128)}), f32[8,1,2,8,4,128]{5,4,3,2,1,0:T(4,128)S(1)}, u32[]{:S(2)}, u32[]{:S(2)}) async-start(f32[8,1,2,8,4,128]{5,4,3,2,1,0:T(4,128)} %fusion.37), calls=%async_computation | async-start | bytes 524288 | tf_op jit(solution)/shard_map/all_to_all | solution.py:105
  52.2 0.2 copy.44
  52.4 0.2 copy.55
  52.6 6.4 %all-to-all-done = f32[8,1,2,8,4,128]{5,4,3,2,1,0:T(4,128)S(1)} async-done(((f32[8,1,2,8,4,128]{5,4,3,2,1,0:T(4,128)}), f32[8,1,2,8,4,128]{5,4,3,2,1,0:T(4,128)S(1)}, u32[]{:S(2)}, u32[]{:S(2)}) %all-to-all-start) | async-done | bytes 262176 | tf_op jit(solution)/shard_map/all_to_all | solution.py:105
  59.0 3.4 %all-to-all-start.3 = ((f32[1,2,8,32,128]{4,2,1,0,3:T(8,128)}), f32[1,2,8,32,128]{4,2,1,0,3:T(8,128)S(1)}, u32[]{:S(2)}, u32[]{:S(2)}) async-start(f32[1,2,8,32,128]{4,2,1,0,3:T(8,128)} %copy.51), calls=%async_computation.3 | async-start | bytes 524288 | tf_op jit(solution)/shard_map/all_to_all | solution.py:112
  62.4 0.2 fusion.32
  62.6 0.2 fusion.15
  62.9 9.8 %all_gather.12 = bf16[2,32,1024]{2,0,1:T(2,128)(2,1)S(1)} all-gather(bf16[2,4,1024]{2,0,1:T(2,128)(2,1)S(1)} %copy.49), channel_id=1, replica_groups=mesh['seq'=8,'head'=4] {'seq'}, dimensions={1}, use_global_device_ids=true | all-gather | bytes 147456 | tf_op jit(solution)/shard_map/all_gather | solution.py:133
  72.7 16.5 %all_gather.13 = bf16[8,32,1024]{2,1,0:T(8,128)(2,1)S(1)} all-gather(bf16[2,32,1024]{2,1,0:T(8,128)(2,1)S(1)} %copy.50), channel_id=1, replica_groups=mesh['seq'=8,'head'=4] {'head'}, dimensions={0}, use_global_device_ids=true | all-gather | bytes 655360 | tf_op jit(solution)/shard_map/all_gather | solution.py:137
  89.2 0.0 all-to-all-done.3
  89.2 0.2 fusion.31
  89.4 0.2 fusion.16
  89.7 9.2 %all_gather.14 = bf16[2,32,1024]{2,0,1:T(2,128)(2,1)S(1)} all-gather(bf16[2,4,1024]{2,0,1:T(2,128)(2,1)S(1)} %copy.60), channel_id=1, replica_groups=mesh['seq'=8,'head'=4] {'seq'}, dimensions={1}, use_global_device_ids=true | all-gather | bytes 147456 | tf_op jit(solution)/shard_map/all_gather | solution.py:134
  98.9 16.5 %all_gather.15 = bf16[8,32,1024]{2,1,0:T(8,128)(2,1)S(1)} all-gather(bf16[2,32,1024]{2,1,0:T(8,128)(2,1)S(1)} %copy.61), channel_id=1, replica_groups=mesh['seq'=8,'head'=4] {'head'}, dimensions={0}, use_global_device_ids=true | all-gather | bytes 655360 | tf_op jit(solution)/shard_map/all_gather | solution.py:138
  115.4 0.1 maximum_bitcast_fusion
  115.5 0.6 copy.62
  116.1 0.5 reshape.152
  116.6 3.0 %fusion = f32[32,2,2048]{2,0,1:T(8,128)S(1)} fusion(bf16[1024,2048]{1,0:T(8,128)(2,1)} %param.15, bf16[32,2,8192]{2,0,1:T(8,128)(2,1)S(1)} %reshape.152, s32[]{:T(128)S(6)} %select_n.47), kind=kOutput, calls=%fused_computation | convolution fusion | flops 268435456 | bytes 4849668 | tf_op jit(solution)/shard_map/nrk,kd->nrd/dot_general | solution.py:148
  119.7 29.5 %all-reduce.2 = bf16[32,2,2048]{2,0,1:T(8,128)(2,1)S(1)} all-reduce(f32[32,2,2048]{2,0,1:T(8,128)S(1)} %fusion), channel_id=2, replica_groups=mesh['seq'=8,'head'=4] {'seq'}, use_global_device_ids=true, to_apply=%region_15.16.clone | all-reduce | flops 131072 | bytes 786432
  149.2 0.6 slice_bitcast_fusion.8
  (29 shorter events, 0.3 us)
Async XLA Ops:
  0.6 1.1 copy-start
  1.7 9.4 %copy-start.4 = (pred[1,2,8,128]{3,1,2,0:T(4,128)(4,1)}, pred[1,2,8,128]{3,1,2,0:T(4,128)(4,1)S(1)}, u32[]{:S(2)}) copy-start(pred[1,2,8,128]{3,1,2,0:T(4,128)(4,1)S(1)} %copy.88) | copy-start | bytes 6148
  1.7 9.4 %copy-start.2 = (bf16[2,2,8,32,128]{4,3,2,1,0:T(8,128)(2,1)S(1)}, bf16[2,2,8,32,128]{4,3,2,1,0:T(8,128)(2,1)}, u32[]{:S(2)}) copy-start(bf16[2,2,8,32,128]{4,3,2,1,0:T(8,128)(2,1)} %param.8) | copy-start | bytes 786436
  3.2 1.4 copy-start.1
  5.2 7.1 %copy-start.3 = (bf16[2,1024,128]{2,1,0:T(8,128)(2,1)S(1)}, bf16[2,1024,128]{2,1,0:T(8,128)(2,1)}, u32[]{:S(2)}) copy-start(bf16[2,1024,128]{2,1,0:T(8,128)(2,1)} %param.12) | copy-start | bytes 1572868
  5.9 17.6 %all-to-all-start.2 = ((f32[1,2,8,32]{2,1,0,3:T(2,128)}), f32[1,2,8,32]{2,1,0,3:T(2,128)}, u32[]{:S(2)}, u32[]{:S(2)}) async-start(f32[1,2,8,32]{2,1,0,3:T(2,128)} %copy.47), calls=%async_computation.2 | async-start | bytes 65536 | tf_op jit(solution)/shard_map/all_to_all | solution.py:103
  14.6 7.1 %copy-start.5 = (bf16[2,2,32,128]{3,2,1,0:T(8,128)(2,1)S(1)}, bf16[2,2,32,128]{3,2,1,0:T(8,128)(2,1)}, u32[]{:S(2)}) copy-start(bf16[2,2,32,128]{3,2,1,0:T(8,128)(2,1)} %param.9) | copy-start | bytes 98308
  21.6 16.0 %copy-start.7 = (u32[32]{0:T(128)S(1)}, u32[32]{0:T(128)}, u32[]{:S(2)}) copy-start(u32[32]{0:T(128)} %constant.61) | copy-start | bytes 388
  23.5 9.0 %all-to-all-start.1 = ((f32[1,2,8,32]{2,1,0,3:T(2,128)}), f32[1,2,8,32]{2,1,0,3:T(2,128)S(1)}, u32[]{:S(2)}, u32[]{:S(2)}) async-start(f32[1,2,8,32]{2,1,0,3:T(2,128)} %copy.42), calls=%async_computation.1 | async-start | bytes 65536 | tf_op jit(solution)/shard_map/all_to_all | solution.py:102
  27.7 35.0 %copy-start.6 = (bf16[2,2,32,128]{3,2,1,0:T(8,128)(2,1)S(1)}, bf16[2,2,32,128]{3,2,1,0:T(8,128)(2,1)}, u32[]{:S(2)}) copy-start(bf16[2,2,32,128]{3,2,1,0:T(8,128)(2,1)} %param.10) | copy-start | bytes 98308
  32.5 8.1 %all-to-all-start.4 = ((f32[1,2,8,32]{2,1,0,3:T(2,128)}), f32[1,2,8,32]{2,1,0,3:T(2,128)S(1)}, u32[]{:S(2)}, u32[]{:S(2)}) async-start(f32[1,2,8,32]{2,1,0,3:T(2,128)} %copy.53), calls=%async_computation.4 | async-start | bytes 65536 | tf_op jit(solution)/shard_map/all_to_all | solution.py:110
  40.6 8.1 %all-to-all-start.5 = ((f32[1,2,8,32]{2,1,0,3:T(2,128)}), f32[1,2,8,32]{2,1,0,3:T(2,128)S(1)}, u32[]{:S(2)}, u32[]{:S(2)}) async-start(f32[1,2,8,32]{2,1,0,3:T(2,128)} %copy.58), calls=%async_computation.5 | async-start | bytes 65536 | tf_op jit(solution)/shard_map/all_to_all | solution.py:111
  48.7 10.3 %all-to-all-start = ((f32[8,1,2,8,4,128]{5,4,3,2,1,0:T(4,128)}), f32[8,1,2,8,4,128]{5,4,3,2,1,0:T(4,128)S(1)}, u32[]{:S(2)}, u32[]{:S(2)}) async-start(f32[8,1,2,8,4,128]{5,4,3,2,1,0:T(4,128)} %fusion.37), calls=%async_computation | async-start | bytes 524288 | tf_op jit(solution)/shard_map/all_to_all | solution.py:105
  59.0 30.2 %all-to-all-start.3 = ((f32[1,2,8,32,128]{4,2,1,0,3:T(8,128)}), f32[1,2,8,32,128]{4,2,1,0,3:T(8,128)S(1)}, u32[]{:S(2)}, u32[]{:S(2)}) async-start(f32[1,2,8,32,128]{4,2,1,0,3:T(8,128)} %copy.51), calls=%async_computation.3 | async-start | bytes 524288 | tf_op jit(solution)/shard_map/all_to_all | solution.py:112
